TPU v7x, 128 devices: a whole 4x4x4 slice. The times are simulated.
128 devices in a mesh: blk: 64 (over y, x_lo, z, core), tile: 2 (over x_hi).
Axes of the slice: x: 4 (x_hi: 2, x_lo: 2; x = x_hi * 2 + x_lo), y: 4, z: 4, core: 2. Of those that a mesh axis runs over, the one named last changes fastest.
Arguments:
- positions: float32 [3, 8192], P(None, ('blk', 'tile')), as said below
- noise_vectors: float32 [3, 32, 8192], P(None, None, ('blk', 'tile')), may hold values from -6 to 6
- spectrum_bounds: float32 [2], replicated, as said below
Outputs:
- displacement: float32 [3, 32, 8192], P(None, None, ('blk', 'tile'))
- images: float32 [2, 3, 32, 8192], P(None, None, None, ('blk', 'tile'))
Inputs may be any that keep to these rules, and one draw needn't show every extreme that they name: `positions`: coordinates lie in a cube whose edge is the cube root of 41.9 * 8192; particle n's third coordinate lies between n and n + 1 times that edge divided by 8192. `spectrum_bounds`: the first entry lies between 0.15 and 0.35; the second exceeds 50 times the first.
All inputs are finite; a program needn't handle non-finite values.
Results may differ from a plain program's by a relative error of at most 0.0003.
Values sent between devices are 32-bit elements; how exact they have to be, the bound alone decides.
A program may use at most 64 MiB of HBM per device.

v0:
```python
import math

import jax
import jax.numpy as jnp
from jax import lax
from jax.experimental import pallas as pl
from jax.experimental.pallas import tpu as pltpu
from jax.sharding import PartitionSpec as P

MESH = pl.DeviceIdType.MESH
F32 = jnp.float32
BF16 = jnp.bfloat16

soft_core = 1e-06
node_count = 32
edge = (41.9 * 8192) ** (1.0 / 3.0)
middle = 0.5 * edge

own = 64
packed = 48
n_src = 8
n_tgt = 16
J = n_src * own

SOURCES = [(0, 0), (1, 0), (3, 0), (0, 1), (2, 0), (1, 1), (3, 1), (2, 1)]


def coords():
    block = lax.axis_index("blk")
    half = lax.axis_index("tile")
    return block // 16, (block // 8) % 2, (block // 2) % 4, block % 2, half


def source_peer(slot):
    dy, flip = SOURCES[slot]
    y, low, z, core, high = coords()
    return ((((y + dy) % 4) * 2 + (low + flip) % 2) * 4 + z) * 2 + core, high


def target_peer(slot):
    quarter = slot // 4
    dz = (2 + 3 * quarter + (quarter // 2) * (3 + 2 * (quarter % 2))) % 4
    flip = 1 - (slot // 2) % 2
    swap = 1 - slot % 2
    y, low, z, core, high = coords()
    return (
        ((y * 2 + (low + flip) % 2) * 4 + (z + dz) % 4) * 2 + (core + swap) % 2,
        (high + flip) % 2,
    )


def remote(src, dst, send, recv, device):
    return pltpu.make_async_remote_copy(
        src_ref=src, dst_ref=dst, send_sem=send, recv_sem=recv, device_id=device, device_id_type=MESH
    )


def lanes(rows):
    return lax.broadcasted_iota(jnp.int32, (rows, 128), 1)


def pack(full):
    tail = full[packed:own]
    moved = jnp.concatenate([pltpu.roll(tail, 96 - 32 * g, 1) if g < 3 else tail for g in range(3)], axis=0)
    return jnp.where(lanes(packed) < 96, full[:packed], moved)


def unpack(block):
    l16 = lanes(16)
    parts = [pltpu.roll(block[16 * g : 16 * g + 16], 32 + 32 * g, 1) for g in range(3)]
    tail = jnp.where(l16 < 32, parts[0], jnp.where(l16 < 64, parts[1], parts[2]))
    return jnp.concatenate([block, tail], axis=0)


def split(value):
    high = value.astype(BF16)
    low = (value - high.astype(F32)).astype(BF16)
    return high, low


def body_kernel(
    pos_ref, noise_ref, bounds_ref, disp_ref, img_ref,
    square, ptile, tpos, spos, srow, scol, tcol, xsrc, xtgt, mats,
    zpk, lpk, field1, field2, rhs, out1, out2, in1, in2,
    tp_send, tp_recv, sp_send, sp_recv, ag1_send, ag1_recv, ag2_send, ag2_recv,
    rs1_send, rs1_recv, rs2_send, rs2_recv,
):
    barrier = pltpu.get_barrier_semaphore()
    for slot in range(n_tgt - 1):
        pl.semaphore_signal(barrier, inc=1, device_id=target_peer(slot), device_id_type=MESH)
    for slot in range(1, n_src):
        pl.semaphore_signal(barrier, inc=1, device_id=source_peer(slot), device_id_type=MESH)

    ptile[...] = jnp.zeros_like(ptile)
    ptile[0:3, 0:own] = pos_ref[...] - middle
    tile = ptile[...]
    tile = tile + pltpu.roll(tile, 64, 1)
    ptile[...] = tile
    tpos[n_tgt - 1] = tile
    spos[0] = tile
    square[...] = jnp.zeros_like(square)
    for a in range(3):
        square[32 * a : 32 * a + 32, 0:own] = noise_ref[a]
    noise = pack(square[...].T[:own])
    zpk[...] = noise
    field1[0] = noise

    pl.semaphore_wait(barrier, n_tgt - 1 + n_src - 1)
    copies = []
    for slot in range(n_src - 1, 0, -1):
        c = remote(ptile, spos.at[slot], sp_send.at[slot], sp_recv.at[slot], source_peer(slot))
        c.start()
        copies.append(c)
    for slot in range(n_tgt - 1):
        there = {1: slot + 4, 2: slot - 4}.get(slot // 4, slot)
        c = remote(ptile, tpos.at[there], tp_send.at[slot], tp_recv.at[there], target_peer(slot))
        c.start()
        copies.append(c)

    def start_gather(block, field, send, recv):
        started = []
        for slot in range(n_src - 1, 0, -1):
            c = remote(block, field.at[slot], send.at[slot], recv.at[slot], source_peer(slot))
            c.start()
            started.append(c)
        return started

    gather1 = start_gather(zpk, field1, ag1_send, ag1_recv)

    lowest = bounds_ref[0]
    highest = bounds_ref[1]
    center = 0.5 * (highest + lowest)
    spread = 0.5 * (highest - lowest)
    q = lanes(8)
    angle = math.pi * (q.astype(F32) + 0.5) / node_count
    cosine = jnp.cos(angle)
    samples = jnp.where(q < node_count, jnp.sqrt(jnp.maximum(center + spread * cosine, 0.0)), 0.0)
    weights = [
        2.0 / node_count * jnp.sum(samples * factor, axis=1, keepdims=True)[0:1]
        for factor in (jnp.ones_like(cosine), cosine, jnp.cos(2.0 * angle))
    ]

    for c in copies:
        c.wait_recv()
    first_half = lanes(8) < own
    for p in range(n_src // 2):
        t = jnp.where(first_half, spos[2 * p], spos[2 * p + 1])
        srow[:, 128 * p : 128 * p + 128] = t
        scol[128 * p : 128 * p + 128, 0:8] = t.T
    for p in range(n_tgt // 2):
        t = jnp.where(first_half, tpos[2 * p], tpos[2 * p + 1])
        tcol[128 * p : 128 * p + 128, 0:8] = t.T

    l16 = lanes(16)

    def pattern(c0, c1, c2, last):
        return jnp.where(l16 < 32, c0, jnp.where(l16 < 64, c1, jnp.where(l16 < 96, c2, last)))

    def source_pattern(step, carry):
        rows = pl.ds(pl.multiple_of(step * 16, 16), 16)
        c = [jnp.broadcast_to(scol[rows, b : b + 1], (16, 128)) for b in range(3)]
        xsrc[rows, :] = pattern(c[0], c[1], c[2], 0.0)
        return carry

    lax.fori_loop(0, J // 16, source_pattern, 0)

    def build(step, carry):
        block = step // 4
        row = (step % 4) * 16
        rows = pl.ds(pl.multiple_of(step * 16, 16), 16)
        c = [jnp.broadcast_to(tcol[rows, b : b + 1], (16, 128)) for b in range(3)]
        xtgt[rows, :] = pattern(c[0], c[1], c[2], -1.0)
        for p in range(J // 128):
            cols = slice(128 * p, 128 * p + 128)
            o = [c[b] - srow[b : b + 1, cols] for b in range(3)]
            squared = o[0] * o[0] + o[1] * o[1] + o[2] * o[2] + soft_core
            inverse = lax.rsqrt(squared)
            inverse2 = inverse * inverse
            near = squared < 4.0
            scalar = jnp.where(near, 1.0 - 0.28125 * (squared * inverse), inverse * (0.75 + 0.5 * inverse2))
            dyadic = inverse * jnp.where(near, 0.09375, inverse2 * (0.75 - 1.5 * inverse2))
            for m, value in enumerate((scalar, dyadic * o[0], dyadic * o[1], dyadic * o[2])):
                high, low = split(value)
                mats[block, pl.ds(pl.multiple_of(m * own + row, 16), 16), cols] = high
                mats[block, pl.ds(pl.multiple_of((4 + m) * own + row, 16), 16), cols] = low
        return carry

    lax.fori_loop(0, n_tgt * 4, build, 0)

    l64 = lanes(own)

    def product(field, gathered, out, into, send, recv):
        for c in gathered:
            c.wait_recv()

        for slot in range(n_src):
            rows = slice(own * slot, own * slot + own)
            u = unpack(field[slot])
            y = u * xsrc[rows, :]
            y = y + pltpu.roll(y, 64, 1)
            y = y + pltpu.roll(y, 32, 1)
            high, low = split(jnp.where(l64 < 96, u, y))
            rhs[rows, 0:128] = high
            rhs[rows, 128:256] = low

        def one_block(slot, carry):
            r = jnp.dot(mats[slot], rhs[...], preferred_element_type=F32)
            r = r[:, 0:128] + r[:, 128:256]
            r = r[: 4 * own] + r[4 * own :]
            x = xtgt[pl.ds(pl.multiple_of(slot * own, own), own), :]
            e = []
            for a in range(3):
                y = r[own * (a + 1) : own * (a + 2)] * x
                e.append(y + pltpu.roll(y, 64, 1))
            here = jnp.where(l64 < 32, e[0], jnp.where(l64 < 64, e[1], e[2]))
            there = jnp.where(l64 < 64, e[0], jnp.where(l64 < 96, e[1], e[2]))
            out[slot] = pack(r[:own] + here + pltpu.roll(there, 96, 1))

            @pl.when(slot < n_tgt - 1)
            def _():
                remote(out.at[slot], into.at[slot], send.at[slot], recv.at[slot], target_peer(slot)).start()

            return carry

        lax.fori_loop(0, n_tgt, one_block, 0)
        total = out[n_tgt - 1]
        for slot in range(n_tgt - 2, -1, -1):
            remote(out.at[slot], into.at[slot], send.at[slot], recv.at[slot], target_peer(slot)).wait_recv()
            total = total + into[slot]
        return total

    def emit(value, store):
        square[0:own, :] = unpack(value)
        turned = square[...].T
        for a in range(3):
            store(a, turned[32 * a : 32 * a + 32, 0:own])

    first = product(field1, gather1, out1, in1, rs1_send, rs1_recv)
    noise = zpk[...]
    linear = (first - center * noise) / spread
    lpk[...] = linear
    field2[0] = linear
    gather2 = start_gather(lpk, field2, ag2_send, ag2_recv)

    def store_first(a, value):
        img_ref[0, a] = value

    emit(first, store_first)

    second = product(field2, gather2, out2, in2, rs2_send, rs2_recv)
    quadratic = 2.0 * (second - center * linear) / spread - noise

    def store_second(a, value):
        img_ref[1, a] = value

    emit(second, store_second)

    def store_disp(a, value):
        disp_ref[a] = value

    emit(0.5 * weights[0] * noise + weights[1] * linear + weights[2] * quadratic, store_disp)

    for c in copies + gather1 + gather2:
        c.wait_send()
    for out, into, send, recv in ((out1, in1, rs1_send, rs1_recv), (out2, in2, rs2_send, rs2_recv)):
        for slot in range(n_tgt - 1):
            remote(out.at[slot], into.at[slot], send.at[slot], recv.at[slot], target_peer(slot)).wait_send()


def body(positions, noise_vectors, spectrum_bounds):
    vmem = pl.BlockSpec(memory_space=pltpu.VMEM)
    dma = pltpu.SemaphoreType.DMA
    return pl.pallas_call(
        body_kernel,
        out_shape=(
            jax.ShapeDtypeStruct((3, 32, own), F32),
            jax.ShapeDtypeStruct((2, 3, 32, own), F32),
        ),
        in_specs=[vmem, vmem, pl.BlockSpec(memory_space=pltpu.SMEM)],
        out_specs=(vmem, vmem),
        scratch_shapes=[
            pltpu.VMEM((128, 128), F32),
            pltpu.VMEM((8, 128), F32),
            pltpu.VMEM((n_tgt, 8, 128), F32),
            pltpu.VMEM((n_src, 8, 128), F32),
            pltpu.VMEM((8, J), F32),
            pltpu.VMEM((J, 128), F32),
            pltpu.VMEM((n_tgt * own, 128), F32),
            pltpu.VMEM((J, 128), F32),
            pltpu.VMEM((n_tgt * own, 128), F32),
            pltpu.VMEM((n_tgt, 8 * own, J), BF16),
            pltpu.VMEM((packed, 128), F32),
            pltpu.VMEM((packed, 128), F32),
            pltpu.VMEM((n_src, packed, 128), F32),
            pltpu.VMEM((n_src, packed, 128), F32),
            pltpu.VMEM((J, 256), BF16),
            pltpu.VMEM((n_tgt, packed, 128), F32),
            pltpu.VMEM((n_tgt, packed, 128), F32),
            pltpu.VMEM((n_tgt, packed, 128), F32),
            pltpu.VMEM((n_tgt, packed, 128), F32),
            dma((n_tgt,)), dma((n_tgt,)), dma((n_src,)), dma((n_src,)),
            dma((n_src,)), dma((n_src,)), dma((n_src,)), dma((n_src,)),
            dma((n_tgt,)), dma((n_tgt,)), dma((n_tgt,)), dma((n_tgt,)),
        ],
        compiler_params=pltpu.CompilerParams(
            collective_id=0, has_side_effects=True, vmem_limit_bytes=40 << 20
        ),
        name="mobility_root",
    )(positions, noise_vectors, spectrum_bounds)


def solution(mesh):
    return jax.shard_map(
        body,
        mesh=mesh,
        in_specs=(P(None, ("blk", "tile")), P(None, None, ("blk", "tile")), P()),
        out_specs=(P(None, None, ("blk", "tile")), P(None, None, None, ("blk", "tile"))),
        check_vma=False,
    )
```

profile of v0, /device:TPU:1, one launch (start us, length us, event | category | flops | bytes accessed | tf_op | source)
XLA Modules:
  0.0 54.6 jit_solution(12251929270695338543)
XLA Ops:
  0.6 0.0 copy-start
  0.6 0.8 %copy-done = f32[3,32,64]{2,1,0:T(8,128)S(1)} copy-done((f32[3,32,64]{2,1,0:T(8,128)S(1)}, f32[3,32,64]{2,1,0:T(8,128)}, u32[]{:S(2)}) %copy-start) | copy-done | bytes 24600
  1.4 0.0 copy-start.1
  1.4 0.7 %copy-done.1 = f32[3,64]{1,0:T(4,128)S(1)} copy-done((f32[3,64]{1,0:T(4,128)S(1)}, f32[3,64]{1,0:T(4,128)}, u32[]{:S(2)}) %copy-start.1) | copy-done | bytes 792
  2.1 0.0 copy-start.2
  2.1 0.7 %copy-done.2 = f32[2]{0:T(128)S(1)} copy-done((f32[2]{0:T(128)S(1)}, f32[2]{0:T(128)}, u32[]{:S(2)}) %copy-start.2) | copy-done | bytes 32
  2.8 50.6 %mobility_root.1 = (f32[3,32,64]{2,1,0:T(8,128)S(1)}, f32[2,3,32,64]{3,2,1,0:T(8,128)S(1)}) custom-call(f32[3,64]{1,0:T(4,128)S(1)} %copy-done.1, f32[3,32,64]{2,1,0:T(8,128)S(1)} %copy-done, f32[2]{0:T(128)S(1)} %copy-done.2), custom_call_target="tpu_custom_call" | custom-call | tf_op jit(solution)/shard_map/mobility_root/pallas_call | solution.py:273
  53.3 0.6 %copy.7 = f32[3,32,64]{2,1,0:T(8,128)} copy(f32[3,32,64]{2,1,0:T(8,128)S(1)} %get-tuple-element.4) | data formatting | bytes 49152
  54.0 0.6 %copy.8 = f32[2,3,32,64]{3,2,1,0:T(8,128)} copy(f32[2,3,32,64]{3,2,1,0:T(8,128)S(1)} %get-tuple-element.5) | data formatting | bytes 98304
Async XLA Ops:
  0.6 0.8 %copy-start = (f32[3,32,64]{2,1,0:T(8,128)S(1)}, f32[3,32,64]{2,1,0:T(8,128)}, u32[]{:S(2)}) copy-start(f32[3,32,64]{2,1,0:T(8,128)} %noise_ref.1) | copy-start | bytes 73732
  1.4 0.7 %copy-start.1 = (f32[3,64]{1,0:T(4,128)S(1)}, f32[3,64]{1,0:T(4,128)}, u32[]{:S(2)}) copy-start(f32[3,64]{1,0:T(4,128)} %pos_ref.1) | copy-start | bytes 2308
  2.1 0.7 %copy-start.2 = (f32[2]{0:T(128)S(1)}, f32[2]{0:T(128)}, u32[]{:S(2)}) copy-start(f32[2]{0:T(128)} %bounds_ref.1) | copy-start | bytes 28
where the time goes:
time: 54.8 us; the launch traced here: 54.6 us
  Pallas kernels  50.6 us (92%)
  local copies, waits for them, and re-layouts  3.39 us (6%)
  between operations  0.65 us (1%)
    pallas_call x1, Pallas kernels, body(): pl.pallas_call(body_kernel, out_shape=(jax.ShapeDtypeStruct((3, 32, own),...  50.6 us
    unnamed x8, local copies, waits for them, and re-layouts  3.39 us

commit v1 on v0

--- a/solution.py
+++ b/solution.py
@@ -79,12 +79,18 @@
 
 
 def body_kernel(
-    pos_ref, noise_ref, bounds_ref, disp_ref, img_ref,
-    square, ptile, tpos, spos, srow, scol, tcol, xsrc, xtgt, mats,
+    pos_hbm, noise_hbm, bounds_hbm, disp_ref, img_ref,
+    pos_ref, noise_ref, bounds_ref, in_sem, square, ptile, tpos, spos, srow, bcol, xsrc, xtgt, mats, raw0, raw1,
     zpk, lpk, field1, field2, rhs, out1, out2, in1, in2,
     tp_send, tp_recv, sp_send, sp_recv, ag1_send, ag1_recv, ag2_send, ag2_recv,
     rs1_send, rs1_recv, rs2_send, rs2_recv,
 ):
+    loads = [
+        pltpu.make_async_copy(src, dst, in_sem.at[k])
+        for k, (src, dst) in enumerate(((pos_hbm, pos_ref), (noise_hbm, noise_ref), (bounds_hbm, bounds_ref)))
+    ]
+    for c in loads:
+        c.start()
     barrier = pltpu.get_barrier_semaphore()
     for slot in range(n_tgt - 1):
         pl.semaphore_signal(barrier, inc=1, device_id=target_peer(slot), device_id_type=MESH)
@@ -92,13 +98,15 @@
         pl.semaphore_signal(barrier, inc=1, device_id=source_peer(slot), device_id_type=MESH)
 
     ptile[...] = jnp.zeros_like(ptile)
+    square[...] = jnp.zeros_like(square)
+    for c in loads:
+        c.wait()
     ptile[0:3, 0:own] = pos_ref[...] - middle
     tile = ptile[...]
     tile = tile + pltpu.roll(tile, 64, 1)
     ptile[...] = tile
     tpos[n_tgt - 1] = tile
     spos[0] = tile
-    square[...] = jnp.zeros_like(square)
     for a in range(3):
         square[32 * a : 32 * a + 32, 0:own] = noise_ref[a]
     noise = pack(square[...].T[:own])
@@ -118,11 +126,11 @@
         copies.append(c)
 
     def start_gather(block, field, send, recv):
-        started = []
+        started = {}
         for slot in range(n_src - 1, 0, -1):
             c = remote(block, field.at[slot], send.at[slot], recv.at[slot], source_peer(slot))
             c.start()
-            started.append(c)
+            started[slot] = c
         return started
 
     gather1 = start_gather(zpk, field1, ag1_send, ag1_recv)
@@ -140,89 +148,101 @@
         for factor in (jnp.ones_like(cosine), cosine, jnp.cos(2.0 * angle))
     ]
 
+    def pattern(c0, c1, c2, last):
+        lane = lanes(c0.shape[0])
+        return jnp.where(lane < 32, c0, jnp.where(lane < 64, c1, jnp.where(lane < 96, c2, last)))
+
     for c in copies:
         c.wait_recv()
     first_half = lanes(8) < own
     for p in range(n_src // 2):
         t = jnp.where(first_half, spos[2 * p], spos[2 * p + 1])
         srow[:, 128 * p : 128 * p + 128] = t
-        scol[128 * p : 128 * p + 128, 0:8] = t.T
+        turned = t.T
+        c = [jnp.broadcast_to(turned[:, b : b + 1], (128, 128)) for b in range(3)]
+        xsrc[128 * p : 128 * p + 128, :] = pattern(*c, 0.0)
     for p in range(n_tgt // 2):
         t = jnp.where(first_half, tpos[2 * p], tpos[2 * p + 1])
-        tcol[128 * p : 128 * p + 128, 0:8] = t.T
-
-    l16 = lanes(16)
-
-    def pattern(c0, c1, c2, last):
-        return jnp.where(l16 < 32, c0, jnp.where(l16 < 64, c1, jnp.where(l16 < 96, c2, last)))
-
-    def source_pattern(step, carry):
-        rows = pl.ds(pl.multiple_of(step * 16, 16), 16)
-        c = [jnp.broadcast_to(scol[rows, b : b + 1], (16, 128)) for b in range(3)]
-        xsrc[rows, :] = pattern(c[0], c[1], c[2], 0.0)
+        turned = t.T
+        c = [jnp.broadcast_to(turned[:, b : b + 1], (128, 128)) for b in range(3)]
+        for b in range(3):
+            bcol[b, 128 * p : 128 * p + 128, :] = c[b]
+        xtgt[128 * p : 128 * p + 128, :] = pattern(*c, -1.0)
+
+    def build(pair, carry):
+        for row in range(0, 2 * own, 16):
+            rows = pl.ds(pl.multiple_of(pair * 2 * own + row, 16), 16)
+            c = [bcol[b, rows, :] for b in range(3)]
+            for p in range(J // 128):
+                cols = slice(128 * p, 128 * p + 128)
+                o = [c[b] - srow[b : b + 1, cols] for b in range(3)]
+                squared = o[0] * o[0] + o[1] * o[1] + o[2] * o[2] + soft_core
+                inverse = lax.rsqrt(squared)
+                inverse2 = inverse * inverse
+                near = squared < 4.0
+                scalar = jnp.where(near, 1.0 - 0.28125 * (squared * inverse), inverse * (0.75 + 0.5 * inverse2))
+                dyadic = inverse * jnp.where(near, 0.09375, inverse2 * (0.75 - 1.5 * inverse2))
+                for m, value in enumerate((scalar, dyadic * o[0], dyadic * o[1], dyadic * o[2])):
+                    high, low = split(value)
+                    at = (row // own * 4 + m) * own + row % own
+                    mats[pair, at : at + 16, cols] = high
+                    mats[pair, at : at + 16, J + 128 * p : J + 128 * p + 128] = low
         return carry
 
-    lax.fori_loop(0, J // 16, source_pattern, 0)
-
-    def build(step, carry):
-        block = step // 4
-        row = (step % 4) * 16
-        rows = pl.ds(pl.multiple_of(step * 16, 16), 16)
-        c = [jnp.broadcast_to(tcol[rows, b : b + 1], (16, 128)) for b in range(3)]
-        xtgt[rows, :] = pattern(c[0], c[1], c[2], -1.0)
-        for p in range(J // 128):
-            cols = slice(128 * p, 128 * p + 128)
-            o = [c[b] - srow[b : b + 1, cols] for b in range(3)]
-            squared = o[0] * o[0] + o[1] * o[1] + o[2] * o[2] + soft_core
-            inverse = lax.rsqrt(squared)
-            inverse2 = inverse * inverse
-            near = squared < 4.0
-            scalar = jnp.where(near, 1.0 - 0.28125 * (squared * inverse), inverse * (0.75 + 0.5 * inverse2))
-            dyadic = inverse * jnp.where(near, 0.09375, inverse2 * (0.75 - 1.5 * inverse2))
-            for m, value in enumerate((scalar, dyadic * o[0], dyadic * o[1], dyadic * o[2])):
-                high, low = split(value)
-                mats[block, pl.ds(pl.multiple_of(m * own + row, 16), 16), cols] = high
-                mats[block, pl.ds(pl.multiple_of((4 + m) * own + row, 16), 16), cols] = low
-        return carry
-
-    lax.fori_loop(0, n_tgt * 4, build, 0)
-
+    lax.fori_loop(0, n_tgt // 2, build, 0)
+
+    raw = (raw0, raw1)
     l64 = lanes(own)
 
     def product(field, gathered, out, into, send, recv):
-        for c in gathered:
-            c.wait_recv()
-
         for slot in range(n_src):
+            if slot:
+                gathered[slot].wait_recv()
             rows = slice(own * slot, own * slot + own)
             u = unpack(field[slot])
             y = u * xsrc[rows, :]
             y = y + pltpu.roll(y, 64, 1)
             y = y + pltpu.roll(y, 32, 1)
             high, low = split(jnp.where(l64 < 96, u, y))
-            rhs[rows, 0:128] = high
-            rhs[rows, 128:256] = low
-
-        def one_block(slot, carry):
-            r = jnp.dot(mats[slot], rhs[...], preferred_element_type=F32)
-            r = r[:, 0:128] + r[:, 128:256]
-            r = r[: 4 * own] + r[4 * own :]
-            x = xtgt[pl.ds(pl.multiple_of(slot * own, own), own), :]
-            e = []
-            for a in range(3):
-                y = r[own * (a + 1) : own * (a + 2)] * x
-                e.append(y + pltpu.roll(y, 64, 1))
-            here = jnp.where(l64 < 32, e[0], jnp.where(l64 < 64, e[1], e[2]))
-            there = jnp.where(l64 < 64, e[0], jnp.where(l64 < 96, e[1], e[2]))
-            out[slot] = pack(r[:own] + here + pltpu.roll(there, 96, 1))
-
-            @pl.when(slot < n_tgt - 1)
-            def _():
-                remote(out.at[slot], into.at[slot], send.at[slot], recv.at[slot], target_peer(slot)).start()
-
-            return carry
-
-        lax.fori_loop(0, n_tgt, one_block, 0)
+            for at in (own * slot, J + own * slot):
+                rhs[at : at + own, 0:128] = high
+                rhs[at : at + own, 128:256] = low
+
+        def multiply(pair):
+            raw[pair % 2][...] = jnp.dot(mats[pair], rhs[...], preferred_element_type=F32)
+
+        lane = lanes(16)
+
+        def rows_of(source, slot, base, g):
+            at = slot * own + 16 * g
+            x = xtgt[at : at + 16, :]
+            r = []
+            for m in range(4):
+                rows = slice(base + own * m + 16 * g, base + own * m + 16 * g + 16)
+                r.append(source[rows, 0:128] + source[rows, 128:256])
+            e = [r[m] * x for m in (1, 2, 3)]
+            e = [v + pltpu.roll(v, 64, 1) for v in e]
+            here = jnp.where(lane < 32, e[0], jnp.where(lane < 64, e[1], e[2]))
+            there = jnp.where(lane < 64, e[0], jnp.where(lane < 96, e[1], e[2]))
+            return r[0] + here + pltpu.roll(there, 96, 1)
+
+        def combine(pair):
+            for half in range(2):
+                slot = 2 * pair + half
+                base = half * 4 * own
+                tail = rows_of(raw[pair % 2], slot, base, 3)
+                for g in range(3):
+                    out[slot, 16 * g : 16 * g + 16, :] = jnp.where(
+                        lane < 96, rows_of(raw[pair % 2], slot, base, g), pltpu.roll(tail, 96 - 32 * g, 1)
+                    )
+                if slot < n_tgt - 1:
+                    remote(out.at[slot], into.at[slot], send.at[slot], recv.at[slot], target_peer(slot)).start()
+
+        multiply(0)
+        for pair in range(1, n_tgt // 2):
+            multiply(pair)
+            combine(pair - 1)
+        combine(n_tgt // 2 - 1)
         total = out[n_tgt - 1]
         for slot in range(n_tgt - 2, -1, -1):
             remote(out.at[slot], into.at[slot], send.at[slot], recv.at[slot], target_peer(slot)).wait_recv()
@@ -260,7 +280,7 @@
 
     emit(0.5 * weights[0] * noise + weights[1] * linear + weights[2] * quadratic, store_disp)
 
-    for c in copies + gather1 + gather2:
+    for c in copies + list(gather1.values()) + list(gather2.values()):
         c.wait_send()
     for out, into, send, recv in ((out1, in1, rs1_send, rs1_recv), (out2, in2, rs2_send, rs2_recv)):
         for slot in range(n_tgt - 1):
@@ -276,24 +296,29 @@
             jax.ShapeDtypeStruct((3, 32, own), F32),
             jax.ShapeDtypeStruct((2, 3, 32, own), F32),
         ),
-        in_specs=[vmem, vmem, pl.BlockSpec(memory_space=pltpu.SMEM)],
+        in_specs=[pl.BlockSpec(memory_space=pl.ANY)] * 3,
         out_specs=(vmem, vmem),
         scratch_shapes=[
+            pltpu.VMEM((3, own), F32),
+            pltpu.VMEM((3, 32, own), F32),
+            pltpu.SMEM((2,), F32),
+            dma((3,)),
             pltpu.VMEM((128, 128), F32),
             pltpu.VMEM((8, 128), F32),
             pltpu.VMEM((n_tgt, 8, 128), F32),
             pltpu.VMEM((n_src, 8, 128), F32),
             pltpu.VMEM((8, J), F32),
+            pltpu.VMEM((3, n_tgt * own, 128), F32),
             pltpu.VMEM((J, 128), F32),
             pltpu.VMEM((n_tgt * own, 128), F32),
-            pltpu.VMEM((J, 128), F32),
-            pltpu.VMEM((n_tgt * own, 128), F32),
-            pltpu.VMEM((n_tgt, 8 * own, J), BF16),
+            pltpu.VMEM((n_tgt // 2, 8 * own, 2 * J), BF16),
+            pltpu.VMEM((8 * own, 256), F32),
+            pltpu.VMEM((8 * own, 256), F32),
             pltpu.VMEM((packed, 128), F32),
             pltpu.VMEM((packed, 128), F32),
             pltpu.VMEM((n_src, packed, 128), F32),
             pltpu.VMEM((n_src, packed, 128), F32),
-            pltpu.VMEM((J, 256), BF16),
+            pltpu.VMEM((2 * J, 256), BF16),
             pltpu.VMEM((n_tgt, packed, 128), F32),
             pltpu.VMEM((n_tgt, packed, 128), F32),
             pltpu.VMEM((n_tgt, packed, 128), F32),

time: 54.8 us -> 46.3 us (0.84)
  Pallas kernels: 50.6 us -> 42.1 us
    pallas_call x1, Pallas kernels: 50.6 us -> 42.1 us  [body(): pl.pallas_call(body_kernel, out_shape=(jax.ShapeDtypeStruct((3, 32, own),...]
where the time goes in v1:
time: 46.3 us; the launch traced here: 46.1 us
  Pallas kernels  42.1 us (91%)
  local copies, waits for them, and re-layouts  3.39 us (7%)
  between operations  0.65 us (1%)
    pallas_call x1, Pallas kernels, body(): pl.pallas_call(body_kernel, out_shape=(jax.ShapeDtypeStruct((3, 32, own),...  42.1 us
    unnamed x8, local copies, waits for them, and re-layouts  3.39 us

profile of v1, /device:TPU:1, one launch (start us, length us, event | category | flops | bytes accessed | tf_op | source)
XLA Modules:
  0.0 46.1 jit_solution(15639486468396488259)
XLA Ops:
  0.6 0.0 copy-start
  0.6 0.8 %copy-done = f32[3,32,64]{2,1,0:T(8,128)S(1)} copy-done((f32[3,32,64]{2,1,0:T(8,128)S(1)}, f32[3,32,64]{2,1,0:T(8,128)}, u32[]{:S(2)}) %copy-start) | copy-done | bytes 24600
  1.4 0.0 copy-start.1
  1.4 0.7 %copy-done.1 = f32[3,64]{1,0:T(4,128)S(1)} copy-done((f32[3,64]{1,0:T(4,128)S(1)}, f32[3,64]{1,0:T(4,128)}, u32[]{:S(2)}) %copy-start.1) | copy-done | bytes 792
  2.1 0.0 copy-start.2
  2.1 0.7 %copy-done.2 = f32[2]{0:T(128)S(1)} copy-done((f32[2]{0:T(128)S(1)}, f32[2]{0:T(128)}, u32[]{:S(2)}) %copy-start.2) | copy-done | bytes 32
  2.8 42.1 %mobility_root.1 = (f32[3,32,64]{2,1,0:T(8,128)S(1)}, f32[2,3,32,64]{3,2,1,0:T(8,128)S(1)}) custom-call(f32[3,64]{1,0:T(4,128)S(1)} %copy-done.1, f32[3,32,64]{2,1,0:T(8,128)S(1)} %copy-done, f32[2]{0:T(128)S(1)} %copy-done.2), custom_call_target="tpu_custom_call" | custom-call | tf_op jit(solution)/shard_map/mobility_root/pallas_call | solution.py:293
  44.9 0.6 %copy.7 = f32[3,32,64]{2,1,0:T(8,128)} copy(f32[3,32,64]{2,1,0:T(8,128)S(1)} %get-tuple-element.4) | data formatting | bytes 49152
  45.5 0.6 %copy.8 = f32[2,3,32,64]{3,2,1,0:T(8,128)} copy(f32[2,3,32,64]{3,2,1,0:T(8,128)S(1)} %get-tuple-element.5) | data formatting | bytes 98304
Async XLA Ops:
  0.6 0.8 %copy-start = (f32[3,32,64]{2,1,0:T(8,128)S(1)}, f32[3,32,64]{2,1,0:T(8,128)}, u32[]{:S(2)}) copy-start(f32[3,32,64]{2,1,0:T(8,128)} %noise_hbm.1) | copy-start | bytes 73732
  1.4 0.7 %copy-start.1 = (f32[3,64]{1,0:T(4,128)S(1)}, f32[3,64]{1,0:T(4,128)}, u32[]{:S(2)}) copy-start(f32[3,64]{1,0:T(4,128)} %pos_hbm.1) | copy-start | bytes 2308
  2.1 0.7 %copy-start.2 = (f32[2]{0:T(128)S(1)}, f32[2]{0:T(128)}, u32[]{:S(2)}) copy-start(f32[2]{0:T(128)} %bounds_hbm.1) | copy-start | bytes 28

commit v2 on v1

v2 whole, which is shorter than its diff:
```python
import math

import jax
import jax.numpy as jnp
from jax import lax
from jax.experimental import pallas as pl
from jax.experimental.pallas import tpu as pltpu
from jax.sharding import PartitionSpec as P

MESH = pl.DeviceIdType.MESH
F32 = jnp.float32
BF16 = jnp.bfloat16

soft_core = 1e-06
node_count = 32
edge = (41.9 * 8192) ** (1.0 / 3.0)
middle = 0.5 * edge

own = 64
packed = 48
n_src = 8
n_tgt = 16
n_pair = n_tgt // 2
J = n_src * own

SOURCES = [(0, 0), (1, 0), (3, 0), (0, 1), (2, 0), (1, 1), (3, 1), (2, 1)]


def coords():
    block = lax.axis_index("blk")
    half = lax.axis_index("tile")
    return block // 16, (block // 8) % 2, (block // 2) % 4, block % 2, half


def source_peer(slot):
    dy, flip = SOURCES[slot]
    y, low, z, core, high = coords()
    return ((((y + dy) % 4) * 2 + (low + flip) % 2) * 4 + z) * 2 + core, high


TARGETS = [(2, 1), (2, 0), (1, 1), (3, 1), (1, 0), (3, 0), (0, 1), (0, 0)]
BACK = [0, 1, 3, 2, 5, 4, 6, 7]


def target_peer(slot):
    dz, flip = TARGETS[slot % n_pair]
    swap = 1 - slot // n_pair
    y, low, z, core, high = coords()
    return (
        ((y * 2 + (low + flip) % 2) * 4 + (z + dz) % 4) * 2 + (core + swap) % 2,
        (high + flip) % 2,
    )


def remote(src, dst, send, recv, device):
    return pltpu.make_async_remote_copy(
        src_ref=src, dst_ref=dst, send_sem=send, recv_sem=recv, device_id=device, device_id_type=MESH
    )


def lanes(rows):
    return lax.broadcasted_iota(jnp.int32, (rows, 128), 1)


def pack(full):
    tail = full[packed:own]
    moved = jnp.concatenate([pltpu.roll(tail, 96 - 32 * g, 1) if g < 3 else tail for g in range(3)], axis=0)
    return jnp.where(lanes(packed) < 96, full[:packed], moved)


def unpack(block):
    l16 = lanes(16)
    parts = [pltpu.roll(block[16 * g : 16 * g + 16], 32 + 32 * g, 1) for g in range(3)]
    tail = jnp.where(l16 < 32, parts[0], jnp.where(l16 < 64, parts[1], parts[2]))
    return jnp.concatenate([block, tail], axis=0)


def split(value):
    high = value.astype(BF16)
    low = (value - high.astype(F32)).astype(BF16)
    return high, low


def body_kernel(
    pos_hbm, noise_hbm, bounds_hbm, disp_ref, img_ref,
    pos_ref, noise_ref, bounds_ref, in_sem, square, ptile, tpos, spos, srow, bcol, xsrc, xtgt, mats, raw0, raw1,
    zpk, lpk, field, rhs, mine, other, into, totals,
    tp_send, tp_recv, sp_send, sp_recv, ag_send, ag_recv, sb_send, sb_recv, rs_send, rs_recv,
):
    loads = [
        pltpu.make_async_copy(src, dst, in_sem.at[k])
        for k, (src, dst) in enumerate(((pos_hbm, pos_ref), (noise_hbm, noise_ref), (bounds_hbm, bounds_ref)))
    ]
    for c in loads:
        c.start()
    barrier = pltpu.get_barrier_semaphore()
    for slot in range(n_tgt - 1):
        pl.semaphore_signal(barrier, inc=1, device_id=target_peer(slot), device_id_type=MESH)
    for slot in range(1, n_src):
        pl.semaphore_signal(barrier, inc=1, device_id=source_peer(slot), device_id_type=MESH)

    ptile[...] = jnp.zeros_like(ptile)
    square[...] = jnp.zeros_like(square)
    for c in loads:
        c.wait()
    ptile[0:3, 0:own] = pos_ref[...] - middle
    tile = ptile[...]
    tile = tile + pltpu.roll(tile, 64, 1)
    ptile[...] = tile
    tpos[n_tgt - 1] = tile
    spos[0] = tile
    for a in range(3):
        square[32 * a : 32 * a + 32, 0:own] = noise_ref[a]
    noise = pack(square[...].T[:own])
    zpk[...] = noise
    field[1, 0] = noise

    raw = (raw0, raw1)
    l64 = lanes(own)

    lane = lanes(16)

    def rows_of(source, slot, base, g):
        x = xtgt[pl.ds(pl.multiple_of(slot * own + 16 * g, 16), 16), :]
        r = []
        for m in range(4):
            rows = slice(base + own * m + 16 * g, base + own * m + 16 * g + 16)
            r.append(source[rows, 0:128] + source[rows, 128:256])
        e = [r[m] * x for m in (1, 2, 3)]
        e = [v + pltpu.roll(v, 64, 1) for v in e]
        here = jnp.where(lane < 32, e[0], jnp.where(lane < 64, e[1], e[2]))
        there = jnp.where(lane < 64, e[0], jnp.where(lane < 96, e[1], e[2]))
        return r[0] + here + pltpu.roll(there, 96, 1)

    def emit(value, store):
        square[0:own, :] = unpack(value)
        turned = square[...].T
        for a in range(3):
            store(a, turned[32 * a : 32 * a + 32, 0:own])

    def gather(phase, block):
        return [
            remote(block, field.at[phase, slot], ag_send.at[phase, slot], ag_recv.at[phase, slot], source_peer(slot))
            for slot in range(n_src - 1, 0, -1)
        ]

    pl.semaphore_wait(barrier, n_tgt - 1 + n_src - 1)
    spread_pos, target_pos = {}, {}
    for slot in range(n_src - 1, 0, -1):
        c = remote(ptile, spos.at[slot], sp_send.at[slot], sp_recv.at[slot], source_peer(slot))
        c.start()
        spread_pos[slot] = c
    for slot in range(n_tgt - 1):
        there = slot // n_pair * n_pair + BACK[slot % n_pair]
        c = remote(ptile, tpos.at[there], tp_send.at[slot], tp_recv.at[there], target_peer(slot))
        c.start()
        target_pos[there] = c

    for c in gather(1, zpk):
        c.start()

    lowest = bounds_ref[0]
    highest = bounds_ref[1]
    center = 0.5 * (highest + lowest)
    spread = 0.5 * (highest - lowest)
    q = lanes(8)
    angle = math.pi * (q.astype(F32) + 0.5) / node_count
    cosine = jnp.cos(angle)
    samples = jnp.where(q < node_count, jnp.sqrt(jnp.maximum(center + spread * cosine, 0.0)), 0.0)
    weights = [
        2.0 / node_count * jnp.sum(samples * factor, axis=1, keepdims=True)[0:1]
        for factor in (jnp.ones_like(cosine), cosine, jnp.cos(2.0 * angle))
    ]

    def pattern(c0, c1, c2, last):
        lane = lanes(c0.shape[0])
        return jnp.where(lane < 32, c0, jnp.where(lane < 64, c1, jnp.where(lane < 96, c2, last)))

    def startup():
        first_half = lanes(8) < own

        def columns(tile):
            turned = tile.T
            return [jnp.broadcast_to(turned[:, b : b + 1], (128, 128)) for b in range(3)]

        def take_source(p):
            for slot in (2 * p, 2 * p + 1):
                if slot:
                    spread_pos[slot].wait_recv()
            tile = jnp.where(first_half, spos[2 * p], spos[2 * p + 1])
            srow[:, 128 * p : 128 * p + 128] = tile
            xsrc[128 * p : 128 * p + 128, :] = pattern(*columns(tile), 0.0)

        def take_target(p):
            for slot in (2 * p, 2 * p + 1):
                if slot < n_tgt - 1:
                    target_pos[slot].wait_recv()
            c = columns(jnp.where(first_half, tpos[2 * p], tpos[2 * p + 1]))
            for b in range(3):
                bcol[b, 128 * p : 128 * p + 128, :] = c[b]
            xtgt[128 * p : 128 * p + 128, :] = pattern(*c, -1.0)

        def build(choose):
            def body(step, carry):
                pair, half = choose(step)
                for row in range(0, 2 * own, 16):
                    rows = pl.ds(pl.multiple_of(pair * 2 * own + row, 16), 16)
                    c = [bcol[b, rows, :] for b in range(3)]
                    for p in range(2):
                        first = pl.multiple_of(half * 256 + 128 * p, 128)
                        cols = pl.ds(first, 128)
                        o = [c[b] - srow[b : b + 1, cols] for b in range(3)]
                        squared = o[0] * o[0] + o[1] * o[1] + o[2] * o[2] + soft_core
                        inverse = lax.rsqrt(squared)
                        inverse2 = inverse * inverse
                        near = squared < 4.0
                        scalar = jnp.where(near, 1.0 - 0.28125 * (squared * inverse), inverse * (0.75 + 0.5 * inverse2))
                        dyadic = inverse * jnp.where(near, 0.09375, inverse2 * (0.75 - 1.5 * inverse2))
                        for m, value in enumerate((scalar, dyadic * o[0], dyadic * o[1], dyadic * o[2])):
                            high, low = split(value)
                            at = (row // own * 4 + m) * own + row % own
                            mats[pair, at : at + 16, cols] = high
                            mats[pair, at : at + 16, pl.ds(pl.multiple_of(J + first, 128), 128)] = low
                return carry

            return body

        for p in (0, 1):
            take_source(p)
        for p in (7, 3, 6, 2):
            take_target(p)
        lax.fori_loop(0, 4, build(lambda step: (step // 2 * 4 + 2 + step % 2, 0)), 0)
        for p in (2, 3):
            take_source(p)
        for p in (5, 4, 1, 0):
            take_target(p)
        lax.fori_loop(0, 12, build(lambda step: (step - step // 8 * (8 - (step - 8) // 2 * 2), 1 - step // 8)), 0)

        for c in list(spread_pos.values()) + list(target_pos.values()):
            c.wait_send()

    def to_sibling(phase, quarter):
        some = pl.ds(quarter * 4, 4)
        return remote(
            mine.at[phase, some], other.at[phase, some], sb_send.at[phase, quarter], sb_recv.at[phase, quarter],
            target_peer(n_pair - 1),
        )

    def to_owner(phase, chip):
        return remote(
            mine.at[phase, n_pair + chip], into.at[phase, chip], rs_send.at[phase, chip], rs_recv.at[phase, chip],
            target_peer(n_pair + chip),
        )

    def one_phase(phase, carry):
        pl.when(phase == 1)(startup)

        def fields_of(slots):
            @pl.when(phase > 0)
            def _():
                for slot, c in zip(range(n_src - 1, 0, -1), gather(phase, zpk)):
                    if slot in slots:
                        c.wait_recv()

            for slot in slots:
                rows = slice(own * slot, own * slot + own)
                u = unpack(field[phase, slot])
                y = u * xsrc[rows, :]
                y = y + pltpu.roll(y, 64, 1)
                y = y + pltpu.roll(y, 32, 1)
                high, low = split(jnp.where(l64 < 96, u, y))
                for at in (own * slot, J + own * slot):
                    rhs[at : at + own, 0:128] = high
                    rhs[at : at + own, 128:256] = low

        fields_of(range(4))
        fields_of(range(4, n_src))

        def multiply(pair, place):
            raw[place][...] = jnp.dot(mats[pair], rhs[...], preferred_element_type=F32)

        def combine(pair, place):
            for half in range(2):
                slot = 2 * pair + half
                base = half * 4 * own
                tail = rows_of(raw[place], slot, base, 3)
                for g in range(3):
                    mine[phase, slot, 16 * g : 16 * g + 16, :] = jnp.where(
                        lane < 96, rows_of(raw[place], slot, base, g), pltpu.roll(tail, 96 - 32 * g, 1)
                    )

        def quarter_of(quarter, carry):
            multiply(2 * quarter, 0)
            multiply(2 * quarter + 1, 1)
            combine(2 * quarter, 0)
            combine(2 * quarter + 1, 1)
            for q in range(2):

                @pl.when((phase > 0) & (quarter == q))
                def _():
                    to_sibling(phase, q).start()

                @pl.when((phase > 0) & (quarter == q + 2))
                def _():
                    to_sibling(phase, q).wait_recv()
                    for chip in range(4 * q, 4 * q + 4):
                        mine[phase, n_pair + chip] = mine[phase, n_pair + chip] + other[phase, chip]
                        if chip < n_pair - 1:
                            to_owner(phase, chip).start()

            return carry

        lax.fori_loop(0, 4, quarter_of, 0)

        @pl.when(phase > 0)
        def _():
            for chip in range(n_pair - 1):
                to_owner(phase, chip).wait_recv()

        total = mine[phase, n_tgt - 1]
        for chip in range(n_pair - 1):
            total = total + into[phase, chip]
        totals[...] = total

        @pl.when(phase == 1)
        def _():
            linear = (total - center * zpk[...]) / spread
            lpk[...] = linear
            field[2, 0] = linear
            for c in gather(2, lpk):
                c.start()

        def store_image(a, value):
            img_ref[phase // 2, a] = value

        emit(total, store_image)

        @pl.when(phase > 0)
        def _():
            for q in range(2):
                to_sibling(phase, q).wait_send()
            for chip in range(n_pair - 1):
                to_owner(phase, chip).wait_send()

        return carry

    lax.fori_loop(1, 3, one_phase, 0)
    noise = zpk[...]
    linear = lpk[...]
    quadratic = 2.0 * (totals[...] - center * linear) / spread - noise

    def store_disp(a, value):
        disp_ref[a] = value

    emit(0.5 * weights[0] * noise + weights[1] * linear + weights[2] * quadratic, store_disp)
    for c in gather(1, zpk) + gather(2, lpk):
        c.wait_send()


def body(positions, noise_vectors, spectrum_bounds):
    vmem = pl.BlockSpec(memory_space=pltpu.VMEM)
    dma = pltpu.SemaphoreType.DMA
    return pl.pallas_call(
        body_kernel,
        out_shape=(
            jax.ShapeDtypeStruct((3, 32, own), F32),
            jax.ShapeDtypeStruct((2, 3, 32, own), F32),
        ),
        in_specs=[pl.BlockSpec(memory_space=pltpu.HBM)] * 3,
        out_specs=(vmem, vmem),
        scratch_shapes=[
            pltpu.VMEM((3, own), F32),
            pltpu.VMEM((3, 32, own), F32),
            pltpu.SMEM((2,), F32),
            dma((3,)),
            pltpu.VMEM((128, 128), F32),
            pltpu.VMEM((8, 128), F32),
            pltpu.VMEM((n_tgt, 8, 128), F32),
            pltpu.VMEM((n_src, 8, 128), F32),
            pltpu.VMEM((8, J), F32),
            pltpu.VMEM((3, n_tgt * own, 128), F32),
            pltpu.VMEM((J, 128), F32),
            pltpu.VMEM((n_tgt * own, 128), F32),
            pltpu.VMEM((n_tgt // 2, 8 * own, 2 * J), BF16),
            pltpu.VMEM((8 * own, 256), F32),
            pltpu.VMEM((8 * own, 256), F32),
            pltpu.VMEM((packed, 128), F32),
            pltpu.VMEM((packed, 128), F32),
            pltpu.VMEM((3, n_src, packed, 128), F32),
            pltpu.VMEM((2 * J, 256), BF16),
            pltpu.VMEM((3, n_tgt, packed, 128), F32),
            pltpu.VMEM((3, n_pair, packed, 128), F32),
            pltpu.VMEM((3, n_pair, packed, 128), F32),
            pltpu.VMEM((packed, 128), F32),
            dma((n_tgt,)), dma((n_tgt,)), dma((n_src,)), dma((n_src,)),
            dma((3, n_src)), dma((3, n_src)), dma((3, 2)), dma((3, 2)),
            dma((3, n_pair)), dma((3, n_pair)),
        ],
        compiler_params=pltpu.CompilerParams(
            collective_id=0, has_side_effects=True, vmem_limit_bytes=64 << 20
        ),
        name="mobility_root",
    )(positions, noise_vectors, spectrum_bounds)


def solution(mesh):
    return jax.shard_map(
        body,
        mesh=mesh,
        in_specs=(P(None, ("blk", "tile")), P(None, None, ("blk", "tile")), P()),
        out_specs=(P(None, None, ("blk", "tile")), P(None, None, None, ("blk", "tile"))),
        check_vma=False,
    )
```

time: 46.3 us -> 43.8 us (0.946)
  Pallas kernels: 42.1 us -> 40.7 us
  local copies, waits for them, and re-layouts: 3.39 us -> 2.1 us
    pallas_call x1, Pallas kernels: 42.1 us -> 40.7 us  [body(): pl.pallas_call(body_kernel, out_shape=(jax.ShapeDtypeStruct((3, 32, own),...]
    unnamed x8 -> x4, local copies, waits for them, and re-layouts: 3.39 us -> 2.1 us
where the time goes in v2:
time: 43.8 us; the launch traced here: 43.4 us
  Pallas kernels  40.7 us (93%)
  local copies, waits for them, and re-layouts  2.1 us (5%)
  between operations  0.65 us (1%)
    pallas_call x1, Pallas kernels, body(): pl.pallas_call(body_kernel, out_shape=(jax.ShapeDtypeStruct((3, 32, own),...  40.7 us
    unnamed x4, local copies, waits for them, and re-layouts  2.1 us

profile of v2, /device:TPU:1, one launch (start us, length us, event | category | flops | bytes accessed | tf_op | source)
XLA Modules:
  0.0 43.4 jit_solution(11174448053160123570)
XLA Ops:
  0.6 40.7 %mobility_root.1 = (f32[3,32,64]{2,1,0:T(8,128)}, f32[2,3,32,64]{3,2,1,0:T(8,128)}) custom-call(f32[3,64]{1,0:T(4,128)} %pos_hbm.1, f32[3,32,64]{2,1,0:T(8,128)} %noise_hbm.1, f32[2]{0:T(128)} %bounds_hbm.1), custom_call_target="tpu_custom_call" | custom-call | tf_op jit(solution)/shard_map/mobility_root/pallas_call | solution.py:363
  41.3 0.0 copy-start
  41.3 1.5 %copy.7 = f32[3,32,64]{2,1,0:T(8,128)} copy(f32[3,32,64]{2,1,0:T(8,128)} %get-tuple-element.4) | data formatting | bytes 49152
  42.8 0.0 copy-done
  42.8 0.6 %copy.8 = f32[2,3,32,64]{3,2,1,0:T(8,128)} copy(f32[2,3,32,64]{3,2,1,0:T(8,128)S(1)} %copy-done) | data formatting | bytes 98304
Async XLA Ops:
  41.3 1.5 %copy-start = (f32[2,3,32,64]{3,2,1,0:T(8,128)S(1)}, f32[2,3,32,64]{3,2,1,0:T(8,128)}, u32[]{:S(2)}) copy-start(f32[2,3,32,64]{3,2,1,0:T(8,128)} %get-tuple-element.5) | copy-start | bytes 147460

commit v3 on v2

--- a/solution.py
+++ b/solution.py
@@ -130,7 +130,7 @@
         e = [v + pltpu.roll(v, 64, 1) for v in e]
         here = jnp.where(lane < 32, e[0], jnp.where(lane < 64, e[1], e[2]))
         there = jnp.where(lane < 64, e[0], jnp.where(lane < 96, e[1], e[2]))
-        return r[0] + here + pltpu.roll(there, 96, 1)
+        return 0.5 * r[0] + here + pltpu.roll(there, 96, 1)
 
     def emit(value, store):
         square[0:own, :] = unpack(value)
@@ -176,6 +176,34 @@
         lane = lanes(c0.shape[0])
         return jnp.where(lane < 32, c0, jnp.where(lane < 64, c1, jnp.where(lane < 96, c2, last)))
 
+    def fill(pair, row, count, p):
+        rows = pl.ds(pair * 2 * own + row, count)
+        c = [bcol[b, rows, :] for b in range(3)]
+        cols = slice(128 * p, 128 * p + 128)
+        o = [c[b] - srow[b : b + 1, cols] for b in range(3)]
+        squared = o[0] * o[0] + o[1] * o[1] + o[2] * o[2] + soft_core
+        inverse = lax.rsqrt(squared)
+        inverse2 = inverse * inverse
+        near = squared < 4.0
+        scalar = jnp.where(near, 2.0 - 0.5625 * (squared * inverse), inverse * (1.5 + inverse2))
+        dyadic = inverse * jnp.where(near, 0.0625, inverse2 * (0.5 - inverse2))
+        for m, value in enumerate((scalar, dyadic * o[0], dyadic * o[1], dyadic * o[2])):
+            high, low = split(value)
+            at = (row // own * 4 + m) * own + row % own
+            mats[pair, at : at + count, cols] = high
+            mats[pair, at : at + count, J + 128 * p : J + 128 * p + 128] = low
+
+    def near_tiles(step, carry):
+        for row in range(0, 2 * own, 64):
+            for p in (0, 1):
+                fill(step // 2 * 4 + 2 + step % 2, row, 64, p)
+        return carry
+
+    def other_tiles(pair):
+        for row in range(0, 2 * own, 64):
+            for p in (range(4) if pair % 4 < 2 else (2, 3)):
+                fill(pair, row, 64, p)
+
     def startup():
         first_half = lanes(8) < own
 
@@ -198,43 +226,17 @@
             c = columns(jnp.where(first_half, tpos[2 * p], tpos[2 * p + 1]))
             for b in range(3):
                 bcol[b, 128 * p : 128 * p + 128, :] = c[b]
-            xtgt[128 * p : 128 * p + 128, :] = pattern(*c, -1.0)
-
-        def build(choose):
-            def body(step, carry):
-                pair, half = choose(step)
-                for row in range(0, 2 * own, 16):
-                    rows = pl.ds(pl.multiple_of(pair * 2 * own + row, 16), 16)
-                    c = [bcol[b, rows, :] for b in range(3)]
-                    for p in range(2):
-                        first = pl.multiple_of(half * 256 + 128 * p, 128)
-                        cols = pl.ds(first, 128)
-                        o = [c[b] - srow[b : b + 1, cols] for b in range(3)]
-                        squared = o[0] * o[0] + o[1] * o[1] + o[2] * o[2] + soft_core
-                        inverse = lax.rsqrt(squared)
-                        inverse2 = inverse * inverse
-                        near = squared < 4.0
-                        scalar = jnp.where(near, 1.0 - 0.28125 * (squared * inverse), inverse * (0.75 + 0.5 * inverse2))
-                        dyadic = inverse * jnp.where(near, 0.09375, inverse2 * (0.75 - 1.5 * inverse2))
-                        for m, value in enumerate((scalar, dyadic * o[0], dyadic * o[1], dyadic * o[2])):
-                            high, low = split(value)
-                            at = (row // own * 4 + m) * own + row % own
-                            mats[pair, at : at + 16, cols] = high
-                            mats[pair, at : at + 16, pl.ds(pl.multiple_of(J + first, 128), 128)] = low
-                return carry
-
-            return body
+            xtgt[128 * p : 128 * p + 128, :] = 1.5 * pattern(*c, -1.0)
 
         for p in (0, 1):
             take_source(p)
         for p in (7, 3, 6, 2):
             take_target(p)
-        lax.fori_loop(0, 4, build(lambda step: (step // 2 * 4 + 2 + step % 2, 0)), 0)
+        lax.fori_loop(0, 4, near_tiles, 0)
         for p in (2, 3):
             take_source(p)
         for p in (5, 4, 1, 0):
             take_target(p)
-        lax.fori_loop(0, 12, build(lambda step: (step - step // 8 * (8 - (step - 8) // 2 * 2), 1 - step // 8)), 0)
 
         for c in list(spread_pos.values()) + list(target_pos.values()):
             c.wait_send()
@@ -253,14 +255,10 @@
         )
 
     def one_phase(phase, carry):
-        pl.when(phase == 1)(startup)
-
         def fields_of(slots):
-            @pl.when(phase > 0)
-            def _():
-                for slot, c in zip(range(n_src - 1, 0, -1), gather(phase, zpk)):
-                    if slot in slots:
-                        c.wait_recv()
+            for slot, c in zip(range(n_src - 1, 0, -1), gather(phase, zpk)):
+                if slot in slots:
+                    c.wait_recv()
 
             for slot in slots:
                 rows = slice(own * slot, own * slot + own)
@@ -289,41 +287,39 @@
                         lane < 96, rows_of(raw[place], slot, base, g), pltpu.roll(tail, 96 - 32 * g, 1)
                     )
 
-        def quarter_of(quarter, carry):
-            multiply(2 * quarter, 0)
-            multiply(2 * quarter + 1, 1)
-            combine(2 * quarter, 0)
-            combine(2 * quarter + 1, 1)
-            for q in range(2):
-
-                @pl.when((phase > 0) & (quarter == q))
-                def _():
-                    to_sibling(phase, q).start()
-
-                @pl.when((phase > 0) & (quarter == q + 2))
-                def _():
-                    to_sibling(phase, q).wait_recv()
-                    for chip in range(4 * q, 4 * q + 4):
-                        mine[phase, n_pair + chip] = mine[phase, n_pair + chip] + other[phase, chip]
-                        if chip < n_pair - 1:
-                            to_owner(phase, chip).start()
-
-            return carry
-
-        lax.fori_loop(0, 4, quarter_of, 0)
-
-        @pl.when(phase > 0)
-        def _():
-            for chip in range(n_pair - 1):
-                to_owner(phase, chip).wait_recv()
+        def exchange(pair):
+            if pair in (1, 3):
+                to_sibling(phase, pair // 2).start()
+            if pair >= 4:
+                if pair % 2 == 0:
+                    to_sibling(phase, (pair - 4) // 2).wait_recv()
+                for chip in (2 * pair - 8, 2 * pair - 7):
+                    mine[phase, n_pair + chip] = mine[phase, n_pair + chip] + other[phase, chip]
+                    if chip < n_pair - 1:
+                        to_owner(phase, chip).start()
+
+        first = phase == 1
+        if first:
+            other_tiles(0)
+        for pair in range(n_pair):
+            multiply(pair, pair % 2)
+            if first and pair + 1 < n_pair:
+                other_tiles(pair + 1)
+            if pair:
+                combine(pair - 1, (pair - 1) % 2)
+                exchange(pair - 1)
+        combine(n_pair - 1, 1)
+        exchange(n_pair - 1)
+
+        for chip in range(n_pair - 1):
+            to_owner(phase, chip).wait_recv()
 
         total = mine[phase, n_tgt - 1]
         for chip in range(n_pair - 1):
             total = total + into[phase, chip]
         totals[...] = total
 
-        @pl.when(phase == 1)
-        def _():
+        if phase == 1:
             linear = (total - center * zpk[...]) / spread
             lpk[...] = linear
             field[2, 0] = linear
@@ -331,20 +327,20 @@
                 c.start()
 
         def store_image(a, value):
-            img_ref[phase // 2, a] = value
+            img_ref[phase - 1, a] = value
 
         emit(total, store_image)
 
-        @pl.when(phase > 0)
-        def _():
-            for q in range(2):
-                to_sibling(phase, q).wait_send()
-            for chip in range(n_pair - 1):
-                to_owner(phase, chip).wait_send()
+        for q in range(2):
+            to_sibling(phase, q).wait_send()
+        for chip in range(n_pair - 1):
+            to_owner(phase, chip).wait_send()
 
         return carry
 
-    lax.fori_loop(1, 3, one_phase, 0)
+    startup()
+    one_phase(1, 0)
+    one_phase(2, 0)
     noise = zpk[...]
     linear = lpk[...]
     quadratic = 2.0 * (totals[...] - center * linear) / spread - noise

time: 43.8 us -> 41.6 us (0.950)
  Pallas kernels: 40.7 us -> 38.7 us
    pallas_call x1, Pallas kernels: 40.7 us -> 38.7 us  [body(): pl.pallas_call(body_kernel, out_shape=(jax.ShapeDtypeStruct((3, 32, own),...]
where the time goes in v3:
time: 41.6 us; the launch traced here: 41.4 us
  Pallas kernels  38.7 us (93%)
  local copies, waits for them, and re-layouts  2.1 us (5%)
  between operations  0.65 us (2%)
    pallas_call x1, Pallas kernels, body(): pl.pallas_call(body_kernel, out_shape=(jax.ShapeDtypeStruct((3, 32, own),...  38.7 us
    unnamed x4, local copies, waits for them, and re-layouts  2.1 us

profile of v3, /device:TPU:1, one launch (start us, length us, event | category | flops | bytes accessed | tf_op | source)
XLA Modules:
  0.0 41.4 jit_solution(9592955895494211175)
XLA Ops:
  0.6 38.7 %mobility_root.1 = (f32[3,32,64]{2,1,0:T(8,128)}, f32[2,3,32,64]{3,2,1,0:T(8,128)}) custom-call(f32[3,64]{1,0:T(4,128)} %pos_hbm.1, f32[3,32,64]{2,1,0:T(8,128)} %noise_hbm.1, f32[2]{0:T(128)} %bounds_hbm.1), custom_call_target="tpu_custom_call" | custom-call | tf_op jit(solution)/shard_map/mobility_root/pallas_call | solution.py:359
  39.3 0.0 copy-start
  39.3 1.5 %copy.7 = f32[3,32,64]{2,1,0:T(8,128)} copy(f32[3,32,64]{2,1,0:T(8,128)} %get-tuple-element.4) | data formatting | bytes 49152
  40.8 0.0 copy-done
  40.8 0.6 %copy.8 = f32[2,3,32,64]{3,2,1,0:T(8,128)} copy(f32[2,3,32,64]{3,2,1,0:T(8,128)S(1)} %copy-done) | data formatting | bytes 98304
Async XLA Ops:
  39.3 1.5 %copy-start = (f32[2,3,32,64]{3,2,1,0:T(8,128)S(1)}, f32[2,3,32,64]{3,2,1,0:T(8,128)}, u32[]{:S(2)}) copy-start(f32[2,3,32,64]{3,2,1,0:T(8,128)} %get-tuple-element.5) | copy-start | bytes 147460

commit v4 on v3

--- a/solution.py
+++ b/solution.py
@@ -271,8 +271,7 @@
                     rhs[at : at + own, 0:128] = high
                     rhs[at : at + own, 128:256] = low
 
-        fields_of(range(4))
-        fields_of(range(4, n_src))
+        fields_of(range(n_src))
 
         def multiply(pair, place):
             raw[place][...] = jnp.dot(mats[pair], rhs[...], preferred_element_type=F32)
@@ -290,10 +289,10 @@
         def exchange(pair):
             if pair in (1, 3):
                 to_sibling(phase, pair // 2).start()
-            if pair >= 4:
-                if pair % 2 == 0:
-                    to_sibling(phase, (pair - 4) // 2).wait_recv()
-                for chip in (2 * pair - 8, 2 * pair - 7):
+            if pair in (5, 7):
+                part = (pair - 5) // 2
+                to_sibling(phase, part).wait_recv()
+                for chip in range(4 * part, 4 * part + 4):
                     mine[phase, n_pair + chip] = mine[phase, n_pair + chip] + other[phase, chip]
                     if chip < n_pair - 1:
                         to_owner(phase, chip).start()
@@ -311,11 +310,10 @@
         combine(n_pair - 1, 1)
         exchange(n_pair - 1)
 
+
+        total = mine[phase, n_tgt - 1]
         for chip in range(n_pair - 1):
             to_owner(phase, chip).wait_recv()
-
-        total = mine[phase, n_tgt - 1]
-        for chip in range(n_pair - 1):
             total = total + into[phase, chip]
         totals[...] = total
 
@@ -326,10 +324,12 @@
             for c in gather(2, lpk):
                 c.start()
 
-        def store_image(a, value):
-            img_ref[phase - 1, a] = value
-
-        emit(total, store_image)
+        if phase == 1:
+
+            def store_image(a, value):
+                img_ref[0, a] = value
+
+            emit(total, store_image)
 
         for q in range(2):
             to_sibling(phase, q).wait_send()
@@ -345,10 +345,13 @@
     linear = lpk[...]
     quadratic = 2.0 * (totals[...] - center * linear) / spread - noise
 
-    def store_disp(a, value):
-        disp_ref[a] = value
-
-    emit(0.5 * weights[0] * noise + weights[1] * linear + weights[2] * quadratic, store_disp)
+    square[0:own, :] = unpack(totals[...])
+    square[own:, :] = unpack(0.5 * weights[0] * noise + weights[1] * linear + weights[2] * quadratic)
+    turned = square[...].T
+    moved = pltpu.roll(turned, 64, 1)
+    for a in range(3):
+        img_ref[1, a] = turned[32 * a : 32 * a + 32, 0:own]
+        disp_ref[a] = moved[32 * a : 32 * a + 32, 0:own]
     for c in gather(1, zpk) + gather(2, lpk):
         c.wait_send()
 

time: 41.6 us -> 41.5 us (level)
  no operation moved by 1% of the time
where the time goes in v4:
time: 41.5 us; the launch traced here: 41.2 us
  Pallas kernels  38.4 us (93%)
  local copies, waits for them, and re-layouts  2.1 us (5%)
  between operations  0.65 us (2%)
    pallas_call x1, Pallas kernels, body(): pl.pallas_call(body_kernel, out_shape=(jax.ShapeDtypeStruct((3, 32, own),...  38.4 us
    unnamed x4, local copies, waits for them, and re-layouts  2.1 us

profile of v4, /device:TPU:1, one launch (start us, length us, event | category | flops | bytes accessed | tf_op | source)
XLA Modules:
  0.0 41.2 jit_solution(712439731742510839)
XLA Ops:
  0.6 38.4 %mobility_root.1 = (f32[3,32,64]{2,1,0:T(8,128)}, f32[2,3,32,64]{3,2,1,0:T(8,128)}) custom-call(f32[3,64]{1,0:T(4,128)} %pos_hbm.1, f32[3,32,64]{2,1,0:T(8,128)} %noise_hbm.1, f32[2]{0:T(128)} %bounds_hbm.1), custom_call_target="tpu_custom_call" | custom-call | tf_op jit(solution)/shard_map/mobility_root/pallas_call | solution.py:362
  39.1 0.0 copy-start
  39.1 1.5 %copy.7 = f32[3,32,64]{2,1,0:T(8,128)} copy(f32[3,32,64]{2,1,0:T(8,128)} %get-tuple-element.4) | data formatting | bytes 49152
  40.5 0.0 copy-done
  40.5 0.6 %copy.8 = f32[2,3,32,64]{3,2,1,0:T(8,128)} copy(f32[2,3,32,64]{3,2,1,0:T(8,128)S(1)} %copy-done) | data formatting | bytes 98304
Async XLA Ops:
  39.1 1.5 %copy-start = (f32[2,3,32,64]{3,2,1,0:T(8,128)S(1)}, f32[2,3,32,64]{3,2,1,0:T(8,128)}, u32[]{:S(2)}) copy-start(f32[2,3,32,64]{3,2,1,0:T(8,128)} %get-tuple-element.5) | copy-start | bytes 147460

commit v5 on v4

--- a/solution.py
+++ b/solution.py
@@ -330,6 +330,9 @@
                 img_ref[0, a] = value
 
             emit(total, store_image)
+            field[0, 0] = (0.5 * weights[0] - weights[2]) * zpk[...] + (
+                weights[1] - 2.0 * center / spread * weights[2]
+            ) * linear
 
         for q in range(2):
             to_sibling(phase, q).wait_send()
@@ -341,12 +344,8 @@
     startup()
     one_phase(1, 0)
     one_phase(2, 0)
-    noise = zpk[...]
-    linear = lpk[...]
-    quadratic = 2.0 * (totals[...] - center * linear) / spread - noise
-
     square[0:own, :] = unpack(totals[...])
-    square[own:, :] = unpack(0.5 * weights[0] * noise + weights[1] * linear + weights[2] * quadratic)
+    square[own:, :] = unpack(field[0, 0] + 2.0 / spread * weights[2] * totals[...])
     turned = square[...].T
     moved = pltpu.roll(turned, 64, 1)
     for a in range(3):

time: 41.5 us -> 41.5 us (level)
  no operation moved by 1% of the time
where the time goes in v5:
time: 41.5 us; the launch traced here: 41.2 us
  Pallas kernels  38.4 us (93%)
  local copies, waits for them, and re-layouts  2.1 us (5%)
  between operations  0.65 us (2%)
    pallas_call x1, Pallas kernels, body(): pl.pallas_call(body_kernel, out_shape=(jax.ShapeDtypeStruct((3, 32, own),...  38.4 us
    unnamed x4, local copies, waits for them, and re-layouts  2.1 us

profile of v5, /device:TPU:1, one launch (start us, length us, event | category | flops | bytes accessed | tf_op | source)
XLA Modules:
  0.0 41.2 jit_solution(5541083728364930796)
XLA Ops:
  0.6 38.4 %mobility_root.1 = (f32[3,32,64]{2,1,0:T(8,128)}, f32[2,3,32,64]{3,2,1,0:T(8,128)}) custom-call(f32[3,64]{1,0:T(4,128)} %pos_hbm.1, f32[3,32,64]{2,1,0:T(8,128)} %noise_hbm.1, f32[2]{0:T(128)} %bounds_hbm.1), custom_call_target="tpu_custom_call" | custom-call | tf_op jit(solution)/shard_map/mobility_root/pallas_call | solution.py:361
  39.1 0.0 copy-start
  39.1 1.5 %copy.7 = f32[3,32,64]{2,1,0:T(8,128)} copy(f32[3,32,64]{2,1,0:T(8,128)} %get-tuple-element.4) | data formatting | bytes 49152
  40.5 0.0 copy-done
  40.5 0.6 %copy.8 = f32[2,3,32,64]{3,2,1,0:T(8,128)} copy(f32[2,3,32,64]{3,2,1,0:T(8,128)S(1)} %copy-done) | data formatting | bytes 98304
Async XLA Ops:
  39.1 1.5 %copy-start = (f32[2,3,32,64]{3,2,1,0:T(8,128)S(1)}, f32[2,3,32,64]{3,2,1,0:T(8,128)}, u32[]{:S(2)}) copy-start(f32[2,3,32,64]{3,2,1,0:T(8,128)} %get-tuple-element.5) | copy-start | bytes 147460
